TPU v7x, 32 devices: a whole 2x2x4 slice. The times are simulated.
32 devices in a mesh: dp: 8 (over z, y), mp: 4 (over x, core).
Axes of the slice: x: 2, y: 2, z: 4, core: 2. Of those that a mesh axis runs over, the one named last changes fastest.
Arguments:
- activations: bfloat16 [4, 4096, 5120], P(None, 'dp'), may hold values from -60 to 60
- task_weights: bfloat16 [4, 5120, 512], P(None, 'dp', 'mp'), may hold values from -6 to 6
Outputs:
- merged: float32 [5120, 512], P('dp', 'mp')
All inputs are finite; a program needn't handle non-finite values.
Results may differ from a plain program's by a relative error of at most 0.0015.
Values may be sent and summed in bfloat16 or wider, within the bound.
A program may use at most 128 MiB of HBM per device.

v0:
```python
import jax
import jax.numpy as jnp
from jax import lax
from jax.sharding import PartitionSpec as P

ALPHA = 0.9


def dot(left, right, dims):
    return lax.dot_general(left, right, (dims, ((), ())), preferred_element_type=jnp.float32)


def rounded(array):
    return lax.reduce_precision(array, 8, 7)


def split_pair(array):
    coarse = rounded(array)
    high = coarse.astype(jnp.bfloat16)
    low = (array - coarse).astype(jnp.bfloat16)
    return jnp.concatenate([high, low], axis=1)


def shards(activations, task_weights):
    tasks, tokens, width = activations.shape
    cols = task_weights.shape[2]
    total = tasks * tokens * lax.axis_size("dp")
    bf16, f32 = (jnp.bfloat16, jnp.float32)
    flat = activations.reshape(tasks * tokens, width)
    weights = lax.all_gather(task_weights, "dp", axis=1, tiled=True)
    squares = jnp.sum(jnp.square(activations.astype(f32)), axis=1)
    squares_all = jnp.sum(squares, axis=0)[:, None]
    mean = jnp.mean(weights.astype(f32), axis=0)
    mean_pair = split_pair(mean)
    gaps = []
    for task in range(tasks):
        wide = dot(
            activations[task], jnp.concatenate([weights[task], mean_pair], axis=1), ((1,), (0,))
        )
        outputs = rounded(wide[:, :cols])
        gaps.append(outputs - (wide[:, cols : 2 * cols] + wide[:, 2 * cols :]))
    gap = split_pair(jnp.concatenate(gaps, axis=0))
    diag = sum((squares[t][:, None] * (weights[t].astype(f32) - mean) for t in range(tasks)))
    inner = dot(flat, gap, ((0,), (0,)))
    inner = inner[:, :cols] + inner[:, cols:]
    residual = lax.psum_scatter(
        (ALPHA * inner + (1.0 - ALPHA) * diag) / total, "dp", scatter_dimension=0, tiled=True
    )
    full_bf = lax.all_gather(residual.astype(bf16), "dp", axis=0, tiled=True)
    full = full_bf.astype(f32)
    projected = split_pair(dot(flat, full_bf, ((1,), (0,))))
    inner = dot(flat, projected, ((0,), (0,)))
    inner = inner[:, :cols] + inner[:, cols:]
    image = lax.psum_scatter(
        (ALPHA * inner + (1.0 - ALPHA) * squares_all * full) / total,
        "dp",
        scatter_dimension=0,
        tiled=True,
    )
    image_full = lax.all_gather(image.astype(bf16), "dp", axis=0, tiled=True).astype(f32)
    norm0 = jnp.sum(full * full, axis=0)
    alpha0 = norm0 / jnp.sum(full * image_full, axis=0)
    next_full = full - alpha0 * image_full
    norm1 = jnp.sum(next_full * next_full, axis=0)
    beta = norm1 / norm0
    direction = next_full + beta * full
    direction_bf = direction.astype(bf16)
    direction = direction_bf.astype(f32)
    projected = dot(flat, direction_bf, ((1,), (0,)))
    energy = lax.psum(
        (
            ALPHA * jnp.sum(projected * projected, axis=0)
            + (1.0 - ALPHA) * jnp.sum(squares_all * direction * direction, axis=0)
        )
        / total,
        "dp",
    )
    alpha1 = norm1 / energy
    own_mean = jnp.mean(task_weights.astype(f32), axis=0)
    return own_mean + alpha0 * residual + alpha1 * (residual - alpha0 * image + beta * residual)


def solution(mesh):
    return jax.shard_map(
        shards,
        mesh=mesh,
        in_specs=(P(None, "dp", None), P(None, "dp", "mp")),
        out_specs=P("dp", "mp"),
        check_vma=False,
    )
```

profile of v0, /device:TPU:0, one launch (start us, length us, event | category | flops | bytes accessed | tf_op | source)
XLA Modules:
  0.0 432.0 jit_solution(4052554290245626200)
XLA Ops:
  6.5 2.2 copy.6
  8.8 9.5 %fusion = (f32[5120]{0:T(1024)S(1)}, f32[4,5120]{1,0:T(4,128)S(1)}) fusion(bf16[4,512,5120]{2,1,0:T(8,128)(2,1)} %param.2), kind=kLoop, calls=%fused_computation.1 | loop fusion | flops 41917440 | bytes 21073920 | tf_op jit(solution)/shard_map/reduce_sum | solution.py:32
  18.9 79.0 %all-gather.4.cloned.1.call-done = bf16[4,5120,128]{1,2,0:T(8,128)(2,1)} async-done(((bf16[4,640,128]{1,2,0:T(8,128)(2,1)}), bf16[4,5120,128]{1,2,0:T(8,128)(2,1)}) %all-gather.4.cloned.1.call-update) | async-done | bytes 5242896 | tf_op jit(solution)/shard_map/all_gather | solution.py:30
  97.9 3.8 convert_reduce_fusion
  102.3 2.1 slice_bitcast_fusion.3
  104.4 6.9 %fusion.30 = f32[512,384]{0,1:T(8,128)} fusion(bf16[4,512,5120]{2,1,0:T(8,128)(2,1)} %param.2, bf16[5120,128]{0,1:T(8,128)(2,1)S(1)} %get-tuple-element.16, bf16[5120,128]{0,1:T(8,128)(2,1)S(1)} %get-tuple-element.15, bf16[5120,128]{0,1:T(8,128)(2,1)} %get-tuple-element.11), kind=kOutput, calls=%fused_computation.65 | convolution fusion | flops 2025062400 | bytes 9961472 | tf_op jit(solution)/shard_map/dot_general | solution.py:10
  112.6 4.7 %fusion.33 = f32[512,384]{0,1:T(8,128)} fusion(bf16[4,512,5120]{2,1,0:T(8,128)(2,1)S(1)} %bitcast.65, bf16[5120,128]{0,1:T(8,128)(2,1)S(1)} %get-tuple-element.16, bf16[5120,128]{0,1:T(8,128)(2,1)S(1)} %get-tuple-element.15, bf16[5120,128]{0,1:T(8,128)(2,1)} %get-tuple-element.14), kind=kOutput, calls=%fused_computation.66 | convolution fusion | flops 2025062400 | bytes 9961472 | tf_op jit(solution)/shard_map/dot_general | solution.py:10
  117.2 3.7 fusion.36
  120.9 3.3 fusion.39
  124.2 1.6 fusion.53
  126.2 7.6 %convolution_bitcast_fusion.1 = f32[5120,256]{0,1:T(8,128)} fusion(bf16[2048,5120]{1,0:T(8,128)(2,1)S(1)} %bitcast.66, bf16[2048,128]{0,1:T(8,128)(2,1)S(1)} %get-tuple-element.20, bf16[2048,128]{0,1:T(8,128)(2,1)S(1)} %get-tuple-element.19), kind=kOutput, calls=%fused_computation.5 | convolution fusion | flops 5370806272 | bytes 27262976 | tf_op jit(solution)/shard_map/dot_general | solution.py:10
  133.8 6.0 %fusion.29 = f32[5120,128]{0,1:T(8,128)} fusion(f32[5120,256]{0,1:T(8,128)} %convolution_bitcast_fusion.1, f32[5120,128]{0,1:T(8,128)S(1)} %convert_reduce_fusion, f32[5120]{0:T(1024)S(1)} %bitcast.68, f32[5120]{0:T(1024)S(1)} %bitcast.69, f32[5120]{0:T(1024)S(1)} %bitcast.70, f32[5120]{0:T(1024)S(1)} %bitcast.67, ...), kind=kLoop, calls=%fused_computation.52 | loop fusion | flops 13762560 | bytes 15810560 | tf_op jit(solution)/shard_map/div | solution.py:47
  139.9 69.6 %reduce-scatter.3.cloned.1.call-done = f32[640,128]{0,1:T(8,128)} async-done(((f32[5120,128]{0,1:T(8,128)}), f32[640,128]{0,1:T(8,128)}) %reduce-scatter.3.cloned.1.call-update) | async-done | bytes 327696 | tf_op jit(solution)/shard_map/reduce_scatter | solution.py:46
  209.4 1.7 convert_element_type.68
  211.2 42.2 %all-gather.6.cloned.1.call-done = bf16[5120,128]{0,1:T(8,128)(2,1)} async-done(((bf16[640,128]{0,1:T(8,128)(2,1)}), bf16[5120,128]{0,1:T(8,128)(2,1)}) %all-gather.6.cloned.1.call-update) | async-done | bytes 1310736 | tf_op jit(solution)/shard_map/all_gather | solution.py:49
  253.4 11.6 %reduce-precision_convert_fusion.1 = (bf16[2048,128]{0,1:T(8,128)(2,1)S(1)}, bf16[2048,128]{0,1:T(8,128)(2,1)S(1)}) fusion(bf16[5120,128]{0,1:T(8,128)(2,1)} %all-gather.6.cloned.1.call-done, bf16[2048,5120]{1,0:T(8,128)(2,1)} %bitcast.61), kind=kOutput, calls=%fused_computation.57 | convolution fusion | flops 2685403136 | bytes 23330816 | tf_op jit(solution)/shard_map/dot_general | solution.py:10
  265.0 10.0 %convolution_bitcast_fusion = f32[5120,256]{0,1:T(8,128)S(1)} fusion(bf16[2048,5120]{1,0:T(8,128)(2,1)} %bitcast.62, bf16[2048,128]{0,1:T(8,128)(2,1)S(1)} %get-tuple-element.18, bf16[2048,128]{0,1:T(8,128)(2,1)S(1)} %get-tuple-element.17), kind=kOutput, calls=%fused_computation.4 | convolution fusion | flops 5370806272 | bytes 27262976 | tf_op jit(solution)/shard_map/dot_general | solution.py:10
  275.0 2.0 fusion.22
  277.1 69.6 %reduce-scatter.5.cloned.1.call-done = f32[640,128]{0,1:T(8,128)} async-done(((f32[5120,128]{0,1:T(8,128)}), f32[640,128]{0,1:T(8,128)}) %reduce-scatter.5.cloned.1.call-update) | async-done | bytes 327696 | tf_op jit(solution)/shard_map/reduce_scatter | solution.py:54
  346.6 1.7 convert_element_type.72
  348.6 41.8 %all-gather.8.cloned.1.call-done = bf16[5120,128]{0,1:T(8,128)(2,1)} async-done(((bf16[640,128]{0,1:T(8,128)(2,1)}), bf16[5120,128]{0,1:T(8,128)(2,1)}) %all-gather.8.cloned.1.call-update) | async-done | bytes 1310736 | tf_op jit(solution)/shard_map/all_gather | solution.py:60
  390.4 2.0 fusion.23
  394.3 11.1 %fusion.42 = f32[128]{0:T(128)S(1)} fusion(bf16[5120,128]{0,1:T(8,128)(2,1)S(1)} %get-tuple-element.10, bf16[2048,5120]{1,0:T(8,128)(2,1)} %bitcast.63), kind=kOutput, calls=%fused_computation.69 | convolution fusion | flops 2684878848 | bytes 22282752 | tf_op jit(solution)/shard_map/dot_general | solution.py:10
  405.4 19.0 %psum.7 = f32[128]{0:T(128)S(1)} all-reduce(f32[128]{0:T(128)S(1)} %add_multiply_fusion), channel_id=1, replica_groups=mesh['dp'=8,'mp'=4] {'dp'}, use_global_device_ids=true, to_apply=%region_11.0 | all-reduce | flops 128 | bytes 1024 | tf_op jit(solution)/shard_map/psum | solution.py:70
  (52 shorter events, 6.2 us)
Async XLA Ops:
  6.5 91.4 %all-gather.4.cloned.1.call-start = ((), (), s32[]{:S(2)}) async-start(), calls=%async_computation.2 | async-start | bytes 5898240 | tf_op jit(solution)/shard_map/all_gather | solution.py:30
  8.8 200.7 %reduce-scatter.3.cloned.1.call-start = ((), (), s32[]{:S(2)}) async-start(), calls=%async_computation.3 | async-start | bytes 2949120 | tf_op jit(solution)/shard_map/reduce_scatter | solution.py:46
  97.9 4.3 copy-start
  101.7 9.5 %slice-start = ((s8[20971520]{0:T(1024)(128)(4,1)}), s8[4194304]{0:T(1024)(128)(4,1)S(1)}, s32[]{:S(2)}) async-start(s8[20971520]{0:T(1024)(128)(4,1)} %bitcast.64), calls=%async_computation.7 | async-start | bytes 8388608
  102.2 9.0 %slice-start.1 = ((s8[20971520]{0:T(1024)(128)(4,1)}), s8[4194304]{0:T(1024)(128)(4,1)S(1)}, s32[]{:S(2)}) async-start(s8[20971520]{0:T(1024)(128)(4,1)} %bitcast.64), calls=%async_computation.8 | async-start | bytes 8388608
  102.3 9.0 %slice-start.2 = ((s8[20971520]{0:T(1024)(128)(4,1)}), s8[4194304]{0:T(1024)(128)(4,1)S(1)}, s32[]{:S(2)}) async-start(s8[20971520]{0:T(1024)(128)(4,1)} %bitcast.64), calls=%async_computation.9 | async-start | bytes 8388608
  104.4 6.9 %slice-start.3 = ((s8[20971520]{0:T(1024)(128)(4,1)}), s8[4194304]{0:T(1024)(128)(4,1)S(1)}, s32[]{:S(2)}) async-start(s8[20971520]{0:T(1024)(128)(4,1)} %bitcast.64), calls=%async_computation.10 | async-start | bytes 8388608
  104.4 8.2 %slice-start.4 = ((s8[20971520]{0:T(1024)(128)(4,1)}), s8[4194304]{0:T(1024)(128)(4,1)S(1)}, s32[]{:S(2)}) async-start(s8[20971520]{0:T(1024)(128)(4,1)} %bitcast.64), calls=%async_computation.11 | async-start | bytes 8388608
  124.2 1.6 copy-start.6
  126.1 7.6 %copy-start.7 = (f32[1,5120]{1,0:T(1,128)S(1)}, f32[1,5120]{1,0:T(1,128)}, u32[]{:S(2)}) copy-start(f32[1,5120]{1,0:T(1,128)} %get-tuple-element.24) | copy-start | bytes 61444
  139.8 113.5 %all-gather.6.cloned.1.call-start = ((), (), s32[]{:S(2)}) async-start(), calls=%async_computation.4 | async-start | bytes 1474560 | tf_op jit(solution)/shard_map/all_gather | solution.py:49
  211.1 135.5 %reduce-scatter.5.cloned.1.call-start = ((), (), s32[]{:S(2)}) async-start(), calls=%async_computation.5 | async-start | bytes 2949120 | tf_op jit(solution)/shard_map/reduce_scatter | solution.py:54
  265.0 10.0 %copy-start.1 = (bf16[5120,128]{0,1:T(8,128)(2,1)S(1)}, bf16[5120,128]{0,1:T(8,128)(2,1)}, u32[]{:S(2)}) copy-start(bf16[5120,128]{0,1:T(8,128)(2,1)} %all-gather.6.cloned.1.call-done) | copy-start | bytes 3932164
  277.0 71.3 %copy-start.3 = (bf16[4,640,128]{2,1,0:T(8,128)(2,1)S(1)}, bf16[4,640,128]{2,1,0:T(8,128)(2,1)}, u32[]{:S(2)}) copy-start(bf16[4,640,128]{2,1,0:T(8,128)(2,1)} %param.3) | copy-start | bytes 1966084
  277.0 113.4 %all-gather.8.cloned.1.call-start = ((), (), s32[]{:S(2)}) async-start(), calls=%async_computation.6 | async-start | bytes 1474560 | tf_op jit(solution)/shard_map/all_gather | solution.py:60
  390.4 2.0 copy-start.2
  394.3 30.2 %copy-start.4 = (f32[640,128]{0,1:T(8,128)S(1)}, f32[640,128]{0,1:T(8,128)}, u32[]{:S(2)}) copy-start(f32[640,128]{0,1:T(8,128)} %reduce-scatter.3.cloned.1.call-done) | copy-start | bytes 983044
  394.3 30.1 %copy-start.5 = (f32[640,128]{0,1:T(8,128)S(1)}, f32[640,128]{0,1:T(8,128)}, u32[]{:S(2)}) copy-start(f32[640,128]{0,1:T(8,128)} %reduce-scatter.5.cloned.1.call-done) | copy-start | bytes 983044
Sparse Core Ops, SparseCore 0:
  9.5 88.3 all-gather.3
  139.9 69.4 reduce-scatter.2
  211.7 41.6 all-gather.5
  277.2 69.4 reduce-scatter.4
  348.7 41.6 all-gather.7
where the time goes:
time: 432 us
  waiting for transfers between devices  302 us (70%)
  matrix products  58.9 us (14%)
  other arithmetic  31.1 us (7%)
  blocking collectives  19 us (4%)
  between operations  13.3 us (3%)
  local copies, waits for them, and re-layouts  7.36 us (2%)
    all_gather x1, waiting for transfers between devices, shards(): weights = lax.all_gather(task_weights, 'dp', axis=1, tiled=True)  79 us
    reduce_scatter x1, waiting for transfers between devices, shards(): lax.psum_scatter((ALPHA * inner + (1.0 - ALPHA) * diag) / total, 'dp', sc...  69.6 us
    reduce_scatter x1, waiting for transfers between devices, shards(): lax.psum_scatter((ALPHA * inner + (1.0 - ALPHA) * squares_all * full) / t...  69.6 us
    dot_general x8, matrix products, dot(): lax.dot_general(left, right, (dims, ((), ())), preferred_element_type=jnp...  58.9 us
    all_gather x1, waiting for transfers between devices, shards(): full_bf = lax.all_gather(residual.astype(bf16), 'dp', axis=0, tiled=True)  42.2 us
    all_gather x1, waiting for transfers between devices, shards(): lax.all_gather(image.astype(bf16), 'dp', axis=0, tiled=True).astype(f32)  41.8 us
    psum x1, blocking collectives, shards(): lax.psum((ALPHA * jnp.sum(projected * projected, axis=0) + (1.0 - ALPHA)...  19 us
    reduce_sum x1, other arithmetic, shards(): squares_all = jnp.sum(squares, axis=0)[:, None]  9.47 us
  transfers between devices with their start and end apart: 5, of which 5 were waited for; matrix products, arithmetic and copies ran while one was open for 2% of the time, Pallas kernels for 0%

commit v1 on v0

--- a/solution.py
+++ b/solution.py
@@ -1,9 +1,29 @@
+import functools
 import jax
 import jax.numpy as jnp
 from jax import lax
 from jax.sharding import PartitionSpec as P
+from jax.lax import axis_index, axis_size, ppermute
 
 ALPHA = 0.9
+
+
+def show_grid_over_axis(original, mesh_name):
+    all_rows = [original]
+    how_many = axis_size(mesh_name)
+    for b in [*range(how_many - 1)]:
+        m_next = ppermute(
+            all_rows[-1],
+            axis_name=mesh_name,
+            perm=[(q, (q + 1) % how_many) for q in range(how_many)],
+        )
+        all_rows.append(m_next)
+    a_now = jnp.concatenate(all_rows[::-1], 1)
+    f_now = axis_index(mesh_name)
+    return jnp.roll(a_now, (f_now + 1) * original.shape[1], 1)
+
+
+launch_knots = functools.partial(show_grid_over_axis, mesh_name="dp")
 
 
 def dot(left, right, dims):
@@ -27,7 +47,7 @@
     total = tasks * tokens * lax.axis_size("dp")
     bf16, f32 = (jnp.bfloat16, jnp.float32)
     flat = activations.reshape(tasks * tokens, width)
-    weights = lax.all_gather(task_weights, "dp", axis=1, tiled=True)
+    weights = launch_knots(task_weights)
     squares = jnp.sum(jnp.square(activations.astype(f32)), axis=1)
     squares_all = jnp.sum(squares, axis=0)[:, None]
     mean = jnp.mean(weights.astype(f32), axis=0)

time: 432 us -> 488 us (1.13)
  waiting for transfers between devices: 302 us -> 328 us
  local copies, waits for them, and re-layouts: 7.36 us -> 30.5 us
    ppermute x0 -> x7, waiting for transfers between devices: none -> 107 us  [show_grid_over_axis(): ppermute(all_rows[-1], axis_name=mesh_name, perm=[(q, (q + 1) % how_many)...]
    all_gather x1 -> x0, waiting for transfers between devices: 79 us -> none  [shards(): weights = lax.all_gather(task_weights, 'dp', axis=1, tiled=True)]
    unnamed x27 -> x44, local copies, waits for them, and re-layouts: 3.55 us -> 20.2 us
    squeeze x1, local copies, waits for them, and re-layouts: 2.09 us -> 7.62 us  [shards(): weights[task]]
  transfers between devices with their start and end apart: 5 -> 11, of which waited for: 5 -> 11; matrix products, arithmetic and copies ran while one was open for 2% -> 2% of each run, Pallas kernels for 0% -> 0%
where the time goes in v1:
time: 488 us; the launch traced here: 487 us
  waiting for transfers between devices  328 us (67%)
  matrix products  59.3 us (12%)
  other arithmetic  34 us (7%)
  local copies, waits for them, and re-layouts  30.5 us (6%)
  blocking collectives  19 us (4%)
  between operations  13.4 us (3%)
    ppermute x7, waiting for transfers between devices, show_grid_over_axis(): ppermute(all_rows[-1], axis_name=mesh_name, perm=[(q, (q + 1) % how_many)...  107 us
    reduce_scatter x1, waiting for transfers between devices, shards(): lax.psum_scatter((ALPHA * inner + (1.0 - ALPHA) * squares_all * full) / t...  69.7 us
    reduce_scatter x1, waiting for transfers between devices, shards(): lax.psum_scatter((ALPHA * inner + (1.0 - ALPHA) * diag) / total, 'dp', sc...  67.2 us
    dot_general x8, matrix products, dot(): lax.dot_general(left, right, (dims, ((), ())), preferred_element_type=jnp...  59.3 us
    all_gather x1, waiting for transfers between devices, shards(): full_bf = lax.all_gather(residual.astype(bf16), 'dp', axis=0, tiled=True)  42 us
    all_gather x1, waiting for transfers between devices, shards(): lax.all_gather(image.astype(bf16), 'dp', axis=0, tiled=True).astype(f32)  41.9 us
    unnamed x44, local copies, waits for them, and re-layouts  20.2 us
    psum x1, blocking collectives, shards(): lax.psum((ALPHA * jnp.sum(projected * projected, axis=0) + (1.0 - ALPHA)...  19 us
  transfers between devices with their start and end apart: 11, of which 11 were waited for; matrix products, arithmetic and copies ran while one was open for 2% of the time, Pallas kernels for 0%

profile of v1, /device:TPU:0, one launch (start us, length us, event | category | flops | bytes accessed | tf_op | source)
XLA Modules:
  0.0 487.3 jit_solution(8937210065055468111)
XLA Ops:
  11.0 17.8 %collective-permute-done = bf16[4,640,128]{1,2,0:T(8,128)(2,1)S(1)} collective-permute-done((bf16[4,640,128]{1,2,0:T(8,128)(2,1)S(1)}, bf16[4,640,128]{1,2,0:T(8,128)(2,1)S(1)}, u32[]{:S(2)}, u32[]{:S(2)}) %collective-permute-start) | collective-permute-done | bytes 655392 | tf_op jit(solution)/shard_map/ppermute | solution.py:15
  28.7 18.6 %collective-permute-done.1 = bf16[4,640,128]{1,2,0:T(8,128)(2,1)S(1)} collective-permute-done((bf16[4,640,128]{1,2,0:T(8,128)(2,1)S(1)}, bf16[4,640,128]{1,2,0:T(8,128)(2,1)S(1)}, u32[]{:S(2)}, u32[]{:S(2)}) %collective-permute-start.1) | collective-permute-done | bytes 655392 | tf_op jit(solution)/shard_map/ppermute | solution.py:15
  47.3 17.7 %collective-permute-done.2 = bf16[4,640,128]{1,2,0:T(8,128)(2,1)S(1)} collective-permute-done((bf16[4,640,128]{1,2,0:T(8,128)(2,1)S(1)}, bf16[4,640,128]{1,2,0:T(8,128)(2,1)S(1)}, u32[]{:S(2)}, u32[]{:S(2)}) %collective-permute-start.2) | collective-permute-done | bytes 655392 | tf_op jit(solution)/shard_map/ppermute | solution.py:15
  65.1 16.9 %collective-permute-done.3 = bf16[4,640,128]{1,2,0:T(8,128)(2,1)S(1)} collective-permute-done((bf16[4,640,128]{1,2,0:T(8,128)(2,1)S(1)}, bf16[4,640,128]{1,2,0:T(8,128)(2,1)S(1)}, u32[]{:S(2)}, u32[]{:S(2)}) %collective-permute-start.3) | collective-permute-done | bytes 655392 | tf_op jit(solution)/shard_map/ppermute | solution.py:15
  82.0 16.1 %collective-permute-done.4 = bf16[4,640,128]{1,2,0:T(8,128)(2,1)} collective-permute-done((bf16[4,640,128]{1,2,0:T(8,128)(2,1)S(1)}, bf16[4,640,128]{1,2,0:T(8,128)(2,1)}, u32[]{:S(2)}, u32[]{:S(2)}) %collective-permute-start.4) | collective-permute-done | bytes 655392 | tf_op jit(solution)/shard_map/ppermute | solution.py:15
  98.1 9.5 %fusion = (f32[5120]{0:T(1024)S(1)}, f32[4,5120]{1,0:T(4,128)S(1)}) fusion(bf16[4,512,5120]{2,1,0:T(8,128)(2,1)} %param.2), kind=kLoop, calls=%fused_computation.1 | loop fusion | flops 41917440 | bytes 21073920 | tf_op jit(solution)/shard_map/reduce_sum | solution.py:52
  107.6 6.0 %collective-permute-done.5 = bf16[4,640,128]{1,2,0:T(8,128)(2,1)} collective-permute-done((bf16[4,640,128]{1,2,0:T(8,128)(2,1)}, bf16[4,640,128]{1,2,0:T(8,128)(2,1)}, u32[]{:S(2)}, u32[]{:S(2)}) %collective-permute-start.5) | collective-permute-done | bytes 655392 | tf_op jit(solution)/shard_map/ppermute | solution.py:15
  114.2 13.9 %collective-permute-done.6 = bf16[4,640,128]{1,2,0:T(8,128)(2,1)S(1)} collective-permute-done((bf16[4,640,128]{1,2,0:T(8,128)(2,1)}, bf16[4,640,128]{1,2,0:T(8,128)(2,1)S(1)}, u32[]{:S(2)}, u32[]{:S(2)}) %collective-permute-start.6) | collective-permute-done | bytes 655392 | tf_op jit(solution)/shard_map/ppermute | solution.py:15
  147.8 5.0 %convert_reduce_fusion = f32[5120,128]{0,1:T(8,128)S(1)} fusion(bf16[4,10240,128]{1,2,0:T(8,128)(2,1)} %constant_dynamic-update-slice_fusion, s32[]{:T(128)S(6)} %select_n.14), kind=kLoop, calls=%fused_computation.3 | loop fusion | flops 4587520 | bytes 7864324 | tf_op jit(solution)/shard_map/reduce_sum | solution.py:53
  154.9 7.6 %dynamic-slice_bitcast_fusion.3 = (bf16[5120,128]{0,1:T(8,128)(2,1)S(1)}, bf16[5120,128]{0,1:T(8,128)(2,1)S(1)}, bf16[5120,128]{0,1:T(8,128)(2,1)S(1)}, bf16[5120,128]{0,1:T(8,128)(2,1)}) fusion(bf16[4,10240,128]{1,2,0:T(8,128)(2,1)} %constant_dynamic-update-slice_fusion, s32[]{:T(128)S(6)} %select_n.14, s32[]{:T(128)S(6)} %add.88, s32[]{:T(128)S(6)} %add.87, ...), kind=kLoop, calls=%fused_computation.63 | loop fusion | bytes 10485776 | tf_op jit(solution)/shard_map/squeeze | solution.py:58
  162.6 5.7 %fusion.30 = f32[512,384]{0,1:T(8,128)} fusion(bf16[4,512,5120]{2,1,0:T(8,128)(2,1)S(1)} %bitcast.57, bf16[5120,128]{0,1:T(8,128)(2,1)} %get-tuple-element.16, bf16[5120,128]{0,1:T(8,128)(2,1)} %get-tuple-element.15, bf16[5120,128]{0,1:T(8,128)(2,1)S(1)} %get-tuple-element.11), kind=kOutput, calls=%fused_computation.65 | convolution fusion | flops 2025062400 | bytes 9961472 | tf_op jit(solution)/shard_map/dot_general | solution.py:30
  168.3 5.2 %fusion.33 = f32[512,384]{0,1:T(8,128)} fusion(bf16[4,512,5120]{2,1,0:T(8,128)(2,1)S(1)} %bitcast.57, bf16[5120,128]{0,1:T(8,128)(2,1)} %get-tuple-element.16, bf16[5120,128]{0,1:T(8,128)(2,1)} %get-tuple-element.15, bf16[5120,128]{0,1:T(8,128)(2,1)} %get-tuple-element.14), kind=kOutput, calls=%fused_computation.66 | convolution fusion | flops 2025062400 | bytes 9961472 | tf_op jit(solution)/shard_map/dot_general | solution.py:30
  173.5 4.2 fusion.36
  177.8 4.1 fusion.39
  184.3 7.5 %convolution_bitcast_fusion.1 = f32[5120,256]{0,1:T(8,128)} fusion(bf16[2048,5120]{1,0:T(8,128)(2,1)S(1)} %bitcast.58, bf16[2048,128]{0,1:T(8,128)(2,1)} %get-tuple-element.20, bf16[2048,128]{0,1:T(8,128)(2,1)S(1)} %get-tuple-element.19), kind=kOutput, calls=%fused_computation.5 | convolution fusion | flops 5370806272 | bytes 27262976 | tf_op jit(solution)/shard_map/dot_general | solution.py:30
  191.8 5.6 %fusion.29 = f32[5120,128]{0,1:T(8,128)} fusion(f32[5120,256]{0,1:T(8,128)} %convolution_bitcast_fusion.1, bf16[5120,128]{0,1:T(8,128)(2,1)} %copy-done.2, bf16[5120,128]{0,1:T(8,128)(2,1)} %copy-done.3, bf16[5120,128]{0,1:T(8,128)(2,1)} %get-tuple-element.14, bf16[5120,128]{0,1:T(8,128)(2,1)S(1)} %get-tuple-element.11, ...), kind=kLoop, calls=%fused_computation.52 | loop fusion | flops 13762560 | bytes 15810560 | tf_op jit(solution)/shard_map/div | solution.py:67
  197.5 67.2 %reduce-scatter.3.cloned.1.call-done = f32[640,128]{0,1:T(8,128)} async-done(((f32[5120,128]{0,1:T(8,128)}), f32[640,128]{0,1:T(8,128)}) %reduce-scatter.3.cloned.1.call-update) | async-done | bytes 327696 | tf_op jit(solution)/shard_map/reduce_scatter | solution.py:66
  266.7 42.0 %all-gather.3.cloned.1.call-done = bf16[5120,128]{0,1:T(8,128)(2,1)} async-done(((bf16[640,128]{0,1:T(8,128)(2,1)}), bf16[5120,128]{0,1:T(8,128)(2,1)}) %all-gather.3.cloned.1.call-update) | async-done | bytes 1310736 | tf_op jit(solution)/shard_map/all_gather | solution.py:69
  308.7 11.4 %reduce-precision_convert_fusion.1 = (bf16[2048,128]{0,1:T(8,128)(2,1)S(1)}, bf16[2048,128]{0,1:T(8,128)(2,1)S(1)}) fusion(bf16[5120,128]{0,1:T(8,128)(2,1)} %all-gather.3.cloned.1.call-done, bf16[2048,5120]{1,0:T(8,128)(2,1)} %bitcast.53), kind=kOutput, calls=%fused_computation.57 | convolution fusion | flops 2685403136 | bytes 23330816 | tf_op jit(solution)/shard_map/dot_general | solution.py:30
  320.1 10.0 %convolution_bitcast_fusion = f32[5120,256]{0,1:T(8,128)S(1)} fusion(bf16[2048,5120]{1,0:T(8,128)(2,1)} %bitcast.54, bf16[2048,128]{0,1:T(8,128)(2,1)S(1)} %get-tuple-element.18, bf16[2048,128]{0,1:T(8,128)(2,1)S(1)} %get-tuple-element.17), kind=kOutput, calls=%fused_computation.4 | convolution fusion | flops 5370806272 | bytes 27262976 | tf_op jit(solution)/shard_map/dot_general | solution.py:30
  332.2 69.7 %reduce-scatter.5.cloned.1.call-done = f32[640,128]{0,1:T(8,128)} async-done(((f32[5120,128]{0,1:T(8,128)}), f32[640,128]{0,1:T(8,128)}) %reduce-scatter.5.cloned.1.call-update) | async-done | bytes 327696 | tf_op jit(solution)/shard_map/reduce_scatter | solution.py:74
  403.9 41.9 %all-gather.5.cloned.1.call-done = bf16[5120,128]{0,1:T(8,128)(2,1)} async-done(((bf16[640,128]{0,1:T(8,128)(2,1)}), bf16[5120,128]{0,1:T(8,128)(2,1)}) %all-gather.5.cloned.1.call-update) | async-done | bytes 1310736 | tf_op jit(solution)/shard_map/all_gather | solution.py:80
  449.6 11.1 %fusion.42 = f32[128]{0:T(128)S(1)} fusion(bf16[5120,128]{0,1:T(8,128)(2,1)S(1)} %get-tuple-element.10, bf16[2048,5120]{1,0:T(8,128)(2,1)} %bitcast.55), kind=kOutput, calls=%fused_computation.69 | convolution fusion | flops 2684878848 | bytes 22282752 | tf_op jit(solution)/shard_map/dot_general | solution.py:30
  460.7 19.0 %psum.7 = f32[128]{0:T(128)S(1)} all-reduce(f32[128]{0:T(128)S(1)} %add_multiply_fusion), channel_id=1, replica_groups=mesh['dp'=8,'mp'=4] {'dp'}, use_global_device_ids=true, to_apply=%region_11.12 | all-reduce | flops 128 | bytes 1024 | tf_op jit(solution)/shard_map/psum | solution.py:90
  (81 shorter events, 40.3 us)
Async XLA Ops:
  6.5 258.2 %reduce-scatter.3.cloned.1.call-start = ((), (), s32[]{:S(2)}) async-start(), calls=%async_computation.2 | async-start | bytes 2949120 | tf_op jit(solution)/shard_map/reduce_scatter | solution.py:66
  7.9 20.8 %collective-permute-start = (bf16[4,640,128]{1,2,0:T(8,128)(2,1)S(1)}, bf16[4,640,128]{1,2,0:T(8,128)(2,1)S(1)}, u32[]{:S(2)}, u32[]{:S(2)}) collective-permute-start(bf16[4,640,128]{1,2,0:T(8,128)(2,1)S(1)} %copy.8), channel_id=1, source_target_pairs={{0,4},{4,8},{8,12},{12,16},{16,20},{20,24},{24,28},{28,0},{1,5},{5... | collective-permute-start | bytes 1966088 | tf_op jit(solution)/shard_map/ppermute | solution.py:15
  28.7 18.6 %collective-permute-start.1 = (bf16[4,640,128]{1,2,0:T(8,128)(2,1)S(1)}, bf16[4,640,128]{1,2,0:T(8,128)(2,1)S(1)}, u32[]{:S(2)}, u32[]{:S(2)}) collective-permute-start(bf16[4,640,128]{1,2,0:T(8,128)(2,1)S(1)} %collective-permute-done), channel_id=1, source_target_pairs={{0,4},{4,8},{8,12},{12,16},{16,20},{20,24},{24,28},{28,0},{1,5},{5... | collective-permute-start | bytes 1966088 | tf_op jit(solution)/shard_map/ppermute | solution.py:15
  47.3 17.7 %collective-permute-start.2 = (bf16[4,640,128]{1,2,0:T(8,128)(2,1)S(1)}, bf16[4,640,128]{1,2,0:T(8,128)(2,1)S(1)}, u32[]{:S(2)}, u32[]{:S(2)}) collective-permute-start(bf16[4,640,128]{1,2,0:T(8,128)(2,1)S(1)} %collective-permute-done.1), channel_id=1, source_target_pairs={{0,4},{4,8},{8,12},{12,16},{16,20},{20,24},{24,28},{28,0},{1,5},{5... | collective-permute-start | bytes 1966088 | tf_op jit(solution)/shard_map/ppermute | solution.py:15
  65.1 16.9 %collective-permute-start.3 = (bf16[4,640,128]{1,2,0:T(8,128)(2,1)S(1)}, bf16[4,640,128]{1,2,0:T(8,128)(2,1)S(1)}, u32[]{:S(2)}, u32[]{:S(2)}) collective-permute-start(bf16[4,640,128]{1,2,0:T(8,128)(2,1)S(1)} %collective-permute-done.2), channel_id=1, source_target_pairs={{0,4},{4,8},{8,12},{12,16},{16,20},{20,24},{24,28},{28,0},{1,5},{5... | collective-permute-start | bytes 1966088 | tf_op jit(solution)/shard_map/ppermute | solution.py:15
  82.0 16.1 %collective-permute-start.4 = (bf16[4,640,128]{1,2,0:T(8,128)(2,1)S(1)}, bf16[4,640,128]{1,2,0:T(8,128)(2,1)}, u32[]{:S(2)}, u32[]{:S(2)}) collective-permute-start(bf16[4,640,128]{1,2,0:T(8,128)(2,1)S(1)} %collective-permute-done.3), channel_id=1, source_target_pairs={{0,4},{4,8},{8,12},{12,16},{16,20},{20,24},{24,28},{28,0},{1,5},{5... | collective-permute-start | bytes 1966088 | tf_op jit(solution)/shard_map/ppermute | solution.py:15
  98.1 15.5 %collective-permute-start.5 = (bf16[4,640,128]{1,2,0:T(8,128)(2,1)}, bf16[4,640,128]{1,2,0:T(8,128)(2,1)}, u32[]{:S(2)}, u32[]{:S(2)}) collective-permute-start(bf16[4,640,128]{1,2,0:T(8,128)(2,1)} %collective-permute-done.4), channel_id=1, source_target_pairs={{0,4},{4,8},{8,12},{12,16},{16,20},{20,24},{24,28},{28,0},{1,5},{5... | collective-permute-start | bytes 1966088 | tf_op jit(solution)/shard_map/ppermute | solution.py:15
  113.6 14.5 %collective-permute-start.6 = (bf16[4,640,128]{1,2,0:T(8,128)(2,1)}, bf16[4,640,128]{1,2,0:T(8,128)(2,1)S(1)}, u32[]{:S(2)}, u32[]{:S(2)}) collective-permute-start(bf16[4,640,128]{1,2,0:T(8,128)(2,1)} %collective-permute-done.5), channel_id=1, source_target_pairs={{0,4},{4,8},{8,12},{12,16},{16,20},{20,24},{24,28},{28,0},{1,5},{5... | collective-permute-start | bytes 1966088 | tf_op jit(solution)/shard_map/ppermute | solution.py:15
  135.0 27.5 %slice-start = ((s8[20971520]{0:T(1024)(128)(4,1)}), s8[4194304]{0:T(1024)(128)(4,1)S(1)}, s32[]{:S(2)}) async-start(s8[20971520]{0:T(1024)(128)(4,1)} %bitcast.56), calls=%async_computation.6 | async-start | bytes 8388608
  140.8 21.7 %slice-start.1 = ((s8[20971520]{0:T(1024)(128)(4,1)}), s8[4194304]{0:T(1024)(128)(4,1)S(1)}, s32[]{:S(2)}) async-start(s8[20971520]{0:T(1024)(128)(4,1)} %bitcast.56), calls=%async_computation.7 | async-start | bytes 8388608
  147.8 14.7 %slice-start.2 = ((s8[20971520]{0:T(1024)(128)(4,1)}), s8[4194304]{0:T(1024)(128)(4,1)S(1)}, s32[]{:S(2)}) async-start(s8[20971520]{0:T(1024)(128)(4,1)} %bitcast.56), calls=%async_computation.8 | async-start | bytes 8388608
  152.8 9.7 %slice-start.3 = ((s8[20971520]{0:T(1024)(128)(4,1)}), s8[4194304]{0:T(1024)(128)(4,1)S(1)}, s32[]{:S(2)}) async-start(s8[20971520]{0:T(1024)(128)(4,1)} %bitcast.56), calls=%async_computation.9 | async-start | bytes 8388608
  154.9 7.7 %slice-start.4 = ((s8[20971520]{0:T(1024)(128)(4,1)}), s8[4194304]{0:T(1024)(128)(4,1)S(1)}, s32[]{:S(2)}) async-start(s8[20971520]{0:T(1024)(128)(4,1)} %bitcast.56), calls=%async_computation.10 | async-start | bytes 8388608
  162.5 11.0 %copy-start.3 = (bf16[5120,128]{0,1:T(8,128)(2,1)}, bf16[5120,128]{0,1:T(8,128)(2,1)S(1)}, u32[]{:S(2)}) copy-start(bf16[5120,128]{0,1:T(8,128)(2,1)S(1)} %get-tuple-element.13) | copy-start | bytes 3932164
  162.5 15.2 %copy-start.2 = (bf16[5120,128]{0,1:T(8,128)(2,1)}, bf16[5120,128]{0,1:T(8,128)(2,1)S(1)}, u32[]{:S(2)}) copy-start(bf16[5120,128]{0,1:T(8,128)(2,1)S(1)} %get-tuple-element.12) | copy-start | bytes 3932164
  177.7 4.1 copy-start.7
  184.3 7.5 %copy-start.8 = (f32[1,5120]{1,0:T(1,128)S(1)}, f32[1,5120]{1,0:T(1,128)}, u32[]{:S(2)}) copy-start(f32[1,5120]{1,0:T(1,128)} %get-tuple-element.24) | copy-start | bytes 61444
  197.4 111.2 %all-gather.3.cloned.1.call-start = ((), (), s32[]{:S(2)}) async-start(), calls=%async_computation.3 | async-start | bytes 1474560 | tf_op jit(solution)/shard_map/all_gather | solution.py:69
  266.4 135.5 %reduce-scatter.5.cloned.1.call-start = ((), (), s32[]{:S(2)}) async-start(), calls=%async_computation.4 | async-start | bytes 2949120 | tf_op jit(solution)/shard_map/reduce_scatter | solution.py:74
  320.1 10.0 %copy-start = (bf16[5120,128]{0,1:T(8,128)(2,1)S(1)}, bf16[5120,128]{0,1:T(8,128)(2,1)}, u32[]{:S(2)}) copy-start(bf16[5120,128]{0,1:T(8,128)(2,1)} %all-gather.3.cloned.1.call-done) | copy-start | bytes 3932164
  332.2 71.5 %copy-start.4 = (bf16[4,640,128]{2,1,0:T(8,128)(2,1)S(1)}, bf16[4,640,128]{2,1,0:T(8,128)(2,1)}, u32[]{:S(2)}) copy-start(bf16[4,640,128]{2,1,0:T(8,128)(2,1)} %param.3) | copy-start | bytes 1966084
  332.2 113.5 %all-gather.5.cloned.1.call-start = ((), (), s32[]{:S(2)}) async-start(), calls=%async_computation.5 | async-start | bytes 1474560 | tf_op jit(solution)/shard_map/all_gather | solution.py:80
  449.6 30.2 %copy-start.5 = (f32[640,128]{0,1:T(8,128)S(1)}, f32[640,128]{0,1:T(8,128)}, u32[]{:S(2)}) copy-start(f32[640,128]{0,1:T(8,128)} %reduce-scatter.3.cloned.1.call-done) | copy-start | bytes 983044
  449.6 30.2 %copy-start.6 = (f32[640,128]{0,1:T(8,128)S(1)}, f32[640,128]{0,1:T(8,128)}, u32[]{:S(2)}) copy-start(f32[640,128]{0,1:T(8,128)} %reduce-scatter.5.cloned.1.call-done) | copy-start | bytes 983044
  (1 other events, 2.0 us)
Sparse Core Ops, SparseCore 0:
  197.6 67.1 reduce-scatter.2
  266.9 41.6 all-gather.2
  332.3 69.5 reduce-scatter.4
  404.0 41.6 all-gather.4
